TPU v7x, 256 devices: a whole 4x4x8 slice. The times are simulated.
256 devices in a mesh: dom: 32 (over z_lo, y, x), ch: 8 (over z_hi, core).
Axes of the slice: x: 4, y: 4, z: 8 (z_hi: 4, z_lo: 2; z = z_hi * 2 + z_lo), core: 2. Of those that a mesh axis runs over, the one named last changes fastest.
Arguments:
- node_feats: bfloat16 [512, 24576], P('ch', 'dom'), may hold values from -6 to 6
- edge_feats: bfloat16 [512, 32768], P('ch', 'dom'), may hold values from -6 to 6
- send_rows: int32 [32768], P('dom'), may hold values from 0 to 767
- edge_src: int32 [32768], P('dom'), may hold values from 0 to 1791
- edge_dst: int32 [32768], P('dom'), may hold values from 0 to 767
- w_edge_in: bfloat16 [2, 3, 512, 512], P(None, None, None, 'ch'), may hold values from -0.15625 to 0.15625
- w_edge_out: bfloat16 [2, 512, 512], P(None, 'ch'), may hold values from -0.25 to 0.25
- w_node_in: bfloat16 [2, 2, 512, 512], P(None, None, None, 'ch'), may hold values from -0.1875 to 0.1875
- w_node_out: bfloat16 [2, 512, 512], P(None, 'ch'), may hold values from -0.25 to 0.25
Outputs:
- nodes_out: bfloat16 [512, 24576], P('ch', 'dom')
- edges_out: bfloat16 [512, 32768], P('ch', 'dom')
All inputs are finite; a program needn't handle non-finite values.
Results may differ from a plain program's by a relative error of at most 0.0085.
Values may be sent and summed in bfloat16 or wider, within the bound.
No kernel may reach another device: no remote copies, remote signals or barrier semaphores. Data moves between devices by JAX's collectives and lax.ppermute only.
A program may use at most 64 MiB of HBM per device.

v0:
```python
import jax
import jax.numpy as jnp
from jax import lax
from jax.sharding import PartitionSpec as P

LATENT = 512
SLOTS = 32
LAYERS = 2


def finish(hidden, weight_out, residual):
    summed = lax.psum_scatter(
        lax.dot_general(
            weight_out, hidden, (((0,), (0,)), ((), ())), preferred_element_type=jnp.float32
        ),
        "ch",
        scatter_dimension=0,
        tiled=True,
    )
    total, squares = lax.psum((jnp.sum(summed, axis=0), jnp.sum(summed * summed, axis=0)), "ch")
    mean = total / LATENT
    var = squares / LATENT - mean * mean
    normed = (summed - mean) * lax.rsqrt(var + 1e-05)
    return (residual.astype(jnp.float32) + normed).astype(jnp.bfloat16)


def edge_hidden(stacked, weight_in):
    return jnp.einsum(
        "akh,ake->he",
        weight_in,
        lax.all_gather(stacked, "ch", axis=1, tiled=True),
        preferred_element_type=jnp.float32,
    )


def shards(
    node_feats,
    edge_feats,
    send_rows,
    edge_src,
    edge_dst,
    w_edge_in,
    w_edge_out,
    w_node_in,
    w_node_out,
):
    share = node_feats.shape[0]
    node_count = node_feats.shape[1]
    domains = lax.axis_size("dom")
    nodes = node_feats
    edges = edge_feats
    for layer in range(LAYERS):
        packed = nodes[:, send_rows].reshape(share, domains, SLOTS)
        received = lax.all_to_all(packed, "dom", split_axis=1, concat_axis=1, tiled=True).reshape(
            share, domains * SLOTS
        )
        extended = jnp.concatenate([nodes, received], axis=1)
        stacked = jnp.stack([edges, extended[:, edge_src], nodes[:, edge_dst]])
        hidden = jax.nn.silu(edge_hidden(stacked, w_edge_in[layer])).astype(jnp.bfloat16)
        edges = finish(hidden, w_edge_out[layer], edges)
        gathered = (
            jnp.zeros((share, node_count), jnp.float32)
            .at[:, edge_dst]
            .add(edges.astype(jnp.float32))
        )
        both = jnp.stack([nodes, gathered.astype(jnp.bfloat16)])
        node_weight = w_node_in[layer]
        hidden_n = jnp.einsum(
            "akh,akn->hn",
            node_weight,
            lax.all_gather(both, "ch", axis=1, tiled=True),
            preferred_element_type=jnp.float32,
        )
        hidden_n = jax.nn.silu(hidden_n).astype(jnp.bfloat16)
        nodes = finish(hidden_n, w_node_out[layer], nodes)
    return (nodes, edges)


def solution(mesh):
    in_specs = (
        P("ch", "dom"),
        P("ch", "dom"),
        P("dom"),
        P("dom"),
        P("dom"),
        P(None, None, None, "ch"),
        P(None, "ch", None),
        P(None, None, None, "ch"),
        P(None, "ch", None),
    )
    out_specs = (P("ch", "dom"), P("ch", "dom"))
    return jax.shard_map(shards, mesh=mesh, in_specs=in_specs, out_specs=out_specs, check_vma=False)
```

profile of v0, /device:TPU:42, one launch (start us, length us, event | category | flops | bytes accessed | tf_op | source)
XLA Modules:
  0.0 487.1 jit_solution(14797563048734557695)
XLA Ops:
  7.2 0.7 fusion.44
  7.9 1.1 copy.23
  8.9 3.2 gather_fusion
  12.2 0.8 reshape.116
  13.0 8.4 %all-to-all-start = ((bf16[32,2,1024]{2,1,0:T(2,128)(2,1)}), bf16[32,2,1024]{2,1,0:T(2,128)(2,1)S(1)}, u32[]{:S(2)}, u32[]{:S(2)}) async-start(bf16[32,2,1024]{2,1,0:T(2,128)(2,1)} %reshape.116), calls=%async_computation | async-start | bytes 262144 | tf_op jit(solution)/shard_map/all_to_all | solution.py:54
  21.5 3.2 gather_fusion.2
  24.7 0.1 copy.29
  24.9 2.0 all-to-all-done
  26.9 0.2 reshape.117
  27.2 3.2 gather_fusion.1
  30.4 0.1 copy.27
  30.6 0.8 pad_maximum_fusion.3
  31.4 43.4 %all-gather.5.cloned.1.call-done = bf16[3,512,1024]{2,1,0:T(8,128)(2,1)} async-done(((bf16[3,64,1024]{2,1,0:T(8,128)(2,1)}), bf16[3,512,1024]{2,1,0:T(8,128)(2,1)}) %all-gather.5.cloned.1.call-update) | async-done | bytes 3145744 | tf_op jit(solution)/shard_map/all_gather | solution.py:31
  74.8 2.9 convolution_bitcast_fusion.1
  77.7 1.9 copy.36
  79.7 0.2 copy.24
  79.9 42.3 %reduce-scatter.13.cloned.1.call-done = f32[64,1024]{1,0:T(8,128)} async-done(((f32[512,1024]{1,0:T(8,128)}), f32[64,1024]{1,0:T(8,128)}) %reduce-scatter.13.cloned.1.call-update) | async-done | bytes 262160
  122.2 1.1 copy.37
  123.3 0.2 multiply_reduce_fusion.1
  123.6 1.0 reduce_sum.72
  124.6 18.0 %all-reduce.3 = (f32[1024]{0:T(1024)S(1)}, f32[1024]{0:T(1024)S(1)}) all-reduce(f32[1024]{0:T(1024)S(1)} %multiply_reduce_fusion.1, f32[1024]{0:T(1024)S(1)} %reduce_sum.72), channel_id=1, replica_groups=mesh['dom'=32,'ch'=8] {'ch'}, use_global_device_ids=true, to_apply=%region_4.5 | all-reduce | flops 2048 | bytes 16384 | tf_op jit(solution)/shard_map/psum | solution.py:20
  142.6 0.3 add_convert_fusion
  142.9 6.2 %scatter_custom_fusion = f32[64,768]{0,1:T(8,128)S(1)} fusion(s32[1024]{0:T(1024)S(1)} %get-tuple-element.23, bf16[64,1024]{0,1:T(8,128)(2,1)S(1)} %add_convert_fusion, f32[]{:T(128)} %constant.23.clone.1), kind=kCustom, calls=%fused_computation.21 | custom fusion | flops 131072 | bytes 458756 | tf_op jit(solution)/shard_map/scatter-add | solution.py:64
  149.2 0.7 pad_maximum_fusion.5
  150.0 33.0 %all-gather.7.cloned.1.call-done = bf16[2,512,768]{2,1,0:T(8,128)(2,1)} async-done(((bf16[2,64,768]{2,1,0:T(8,128)(2,1)}), bf16[2,512,768]{2,1,0:T(8,128)(2,1)}) %all-gather.7.cloned.1.call-update) | async-done | bytes 1572880 | tf_op jit(solution)/shard_map/all_gather | solution.py:71
  183.0 2.2 convolution_bitcast_fusion.3
  185.2 1.6 copy.38
  186.8 39.2 %reduce-scatter.15.cloned.1.call-done = f32[64,768]{1,0:T(8,128)} async-done(((f32[512,768]{1,0:T(8,128)}), f32[64,768]{1,0:T(8,128)}) %reduce-scatter.15.cloned.1.call-update) | async-done | bytes 196624
  226.0 1.1 copy.39
  227.1 0.2 multiply_reduce_fusion.3
  227.3 1.0 reduce_sum.74
  228.2 16.3 %all-reduce.2 = (f32[768]{0:T(1024)S(1)}, f32[768]{0:T(1024)S(1)}) all-reduce(f32[768]{0:T(1024)S(1)} %multiply_reduce_fusion.3, f32[768]{0:T(1024)S(1)} %reduce_sum.74), channel_id=1, replica_groups=mesh['dom'=32,'ch'=8] {'ch'}, use_global_device_ids=true, to_apply=%region_10.11 | all-reduce | flops 1536 | bytes 12288 | tf_op jit(solution)/shard_map/psum | solution.py:20
  244.6 0.3 add_convert_fusion.2
  244.9 3.2 gather_fusion.3
  248.1 0.8 reshape.118
  248.9 8.5 %all-to-all-start.1 = ((bf16[32,2,1024]{2,1,0:T(2,128)(2,1)}), bf16[32,2,1024]{2,1,0:T(2,128)(2,1)S(1)}, u32[]{:S(2)}, u32[]{:S(2)}) async-start(bf16[32,2,1024]{2,1,0:T(2,128)(2,1)} %reshape.118), calls=%async_computation.1 | async-start | bytes 262144 | tf_op jit(solution)/shard_map/all_to_all | solution.py:54
  257.5 3.2 gather_fusion.5
  260.7 2.2 all-to-all-done.1
  262.9 0.2 reshape.119
  263.2 3.2 gather_fusion.4
  266.4 0.2 pad_maximum_fusion
  266.6 1.0 copy.31
  267.7 41.0 %all-gather.9.cloned.1.call-done = bf16[3,512,1024]{2,1,0:T(8,128)(2,1)} async-done(((bf16[3,64,1024]{2,1,0:T(8,128)(2,1)}), bf16[3,512,1024]{2,1,0:T(8,128)(2,1)}) %all-gather.9.cloned.1.call-update) | async-done | bytes 3145744 | tf_op jit(solution)/shard_map/all_gather | solution.py:31
  308.7 2.9 convolution_bitcast_fusion
  311.6 1.9 copy.40
  313.5 42.5 %reduce-scatter.17.cloned.1.call-done = f32[64,1024]{1,0:T(8,128)} async-done(((f32[512,1024]{1,0:T(8,128)}), f32[64,1024]{1,0:T(8,128)}) %reduce-scatter.17.cloned.1.call-update) | async-done | bytes 262160
  356.1 1.1 copy.41
  357.2 0.2 multiply_reduce_fusion
  357.4 1.0 reduce_sum.76
  358.4 18.4 %all-reduce.1 = (f32[1024]{0:T(1024)S(1)}, f32[1024]{0:T(1024)S(1)}) all-reduce(f32[1024]{0:T(1024)S(1)} %multiply_reduce_fusion, f32[1024]{0:T(1024)S(1)} %reduce_sum.76), channel_id=1, replica_groups=mesh['dom'=32,'ch'=8] {'ch'}, use_global_device_ids=true, to_apply=%region_15.16 | all-reduce | flops 2048 | bytes 16384 | tf_op jit(solution)/shard_map/psum | solution.py:20
  376.8 0.3 fusion.6
  377.2 6.2 %scatter_custom_fusion.1 = f32[64,768]{0,1:T(8,128)S(1)} fusion(s32[1024]{0:T(1024)S(1)} %get-tuple-element.23, bf16[64,1024]{0,1:T(8,128)(2,1)S(1)} %fusion.6, f32[]{:T(128)} %constant.23.clone.1), kind=kCustom, calls=%fused_computation.23 | custom fusion | flops 131072 | bytes 458756 | tf_op jit(solution)/shard_map/scatter-add | solution.py:64
  383.5 0.9 copy.32
  384.4 32.9 %all-gather.11.cloned.1.call-done = bf16[2,512,768]{2,0,1:T(2,128)(2,1)} async-done(((bf16[2,64,768]{2,0,1:T(2,128)(2,1)}), bf16[2,512,768]{2,0,1:T(2,128)(2,1)}) %all-gather.11.cloned.1.call-update) | async-done | bytes 1572880 | tf_op jit(solution)/shard_map/all_gather | solution.py:71
  417.3 2.2 convolution_bitcast_fusion.2
  419.5 1.6 copy.42
  421.1 0.8 copy.35
  421.9 38.7 %reduce-scatter.19.cloned.1.call-done = f32[64,768]{1,0:T(8,128)} async-done(((f32[512,768]{1,0:T(8,128)}), f32[64,768]{1,0:T(8,128)}) %reduce-scatter.19.cloned.1.call-update) | async-done | bytes 196624
  460.6 1.1 copy.43
  461.7 0.2 multiply_reduce_fusion.2
  461.9 1.0 reduce_sum.78
  462.8 16.3 %all-reduce = (f32[768]{0:T(1024)S(1)}, f32[768]{0:T(1024)S(1)}) all-reduce(f32[768]{0:T(1024)S(1)} %multiply_reduce_fusion.2, f32[768]{0:T(1024)S(1)} %reduce_sum.78), channel_id=1, replica_groups=mesh['dom'=32,'ch'=8] {'ch'}, use_global_device_ids=true, to_apply=%region_21.22 | all-reduce | flops 1536 | bytes 12288 | tf_op jit(solution)/shard_map/psum | solution.py:20
  479.2 0.3 add_convert_fusion.1
  479.4 0.8 copy.34
  (45 shorter events, 1.0 us)
Async XLA Ops:
  7.2 14.3 %copy-start.7 = (s32[1024]{0:T(1024)S(1)}, s32[1024]{0:T(1024)}, u32[]{:S(2)}) copy-start(s32[1024]{0:T(1024)} %param.13) | copy-start | bytes 12292
  8.9 16.0 %copy-start.8 = (s32[1024]{0:T(1024)S(1)}, s32[1024]{0:T(1024)}, u32[]{:S(2)}) copy-start(s32[1024]{0:T(1024)} %param.12) | copy-start | bytes 12292
  13.0 13.9 %all-to-all-start = ((bf16[32,2,1024]{2,1,0:T(2,128)(2,1)}), bf16[32,2,1024]{2,1,0:T(2,128)(2,1)S(1)}, u32[]{:S(2)}, u32[]{:S(2)}) async-start(bf16[32,2,1024]{2,1,0:T(2,128)(2,1)} %reshape.116), calls=%async_computation | async-start | bytes 262144 | tf_op jit(solution)/shard_map/all_to_all | solution.py:54
  21.4 53.4 %all-gather.5.cloned.1.call-start = ((), (), s32[]{:S(2)}) async-start(), calls=%async_computation.6 | async-start | bytes 3538944 | tf_op jit(solution)/shard_map/all_gather | solution.py:31
  24.7 5.8 %copy-start = (bf16[64,1024]{1,0:T(8,128)(2,1)S(1)}, bf16[64,1024]{1,0:T(8,128)(2,1)}, u32[]{:S(2)}) copy-start(bf16[64,1024]{1,0:T(8,128)(2,1)} %param.10) | copy-start | bytes 393220
  27.2 47.6 %copy-start.1 = (bf16[2,3,512,64]{2,3,1,0:T(8,128)(2,1)S(1)}, bf16[2,3,512,64]{2,3,1,0:T(8,128)(2,1)}, u32[]{:S(2)}) copy-start(bf16[2,3,512,64]{2,3,1,0:T(8,128)(2,1)} %param.14) | copy-start | bytes 1179652
  27.2 47.6 %copy-start.4 = (bf16[2,64,512]{2,1,0:T(8,128)(2,1)S(1)}, bf16[2,64,512]{2,1,0:T(8,128)(2,1)}, u32[]{:S(2)}) copy-start(bf16[2,64,512]{2,1,0:T(8,128)(2,1)} %param.15) | copy-start | bytes 393220
  31.4 90.8 %reduce-scatter.13.cloned.1.call-start = ((), (), s32[]{:S(2)}) async-start(), calls=%async_computation.10 | async-start | bytes 2359296
  79.6 103.3 %all-gather.7.cloned.1.call-start = ((), (), s32[]{:S(2)}) async-start(), calls=%async_computation.7 | async-start | bytes 1769472 | tf_op jit(solution)/shard_map/all_gather | solution.py:71
  123.3 25.9 %copy-start.2 = (bf16[64,768]{1,0:T(8,128)(2,1)S(1)}, bf16[64,768]{1,0:T(8,128)(2,1)}, u32[]{:S(2)}) copy-start(bf16[64,768]{1,0:T(8,128)(2,1)} %param.9) | copy-start | bytes 294916
  123.5 59.4 %copy-start.3 = (bf16[2,2,512,64]{2,3,1,0:T(8,128)(2,1)S(1)}, bf16[2,2,512,64]{2,3,1,0:T(8,128)(2,1)}, u32[]{:S(2)}) copy-start(bf16[2,2,512,64]{2,3,1,0:T(8,128)(2,1)} %param.16) | copy-start | bytes 786436
  123.5 59.4 %copy-start.5 = (bf16[2,64,512]{2,1,0:T(8,128)(2,1)S(1)}, bf16[2,64,512]{2,1,0:T(8,128)(2,1)}, u32[]{:S(2)}) copy-start(bf16[2,64,512]{2,1,0:T(8,128)(2,1)} %param.17) | copy-start | bytes 393220
  149.9 76.0 %reduce-scatter.15.cloned.1.call-start = ((), (), s32[]{:S(2)}) async-start(), calls=%async_computation.11 | async-start | bytes 1769472
  248.9 13.9 %all-to-all-start.1 = ((bf16[32,2,1024]{2,1,0:T(2,128)(2,1)}), bf16[32,2,1024]{2,1,0:T(2,128)(2,1)S(1)}, u32[]{:S(2)}, u32[]{:S(2)}) async-start(bf16[32,2,1024]{2,1,0:T(2,128)(2,1)} %reshape.118), calls=%async_computation.1 | async-start | bytes 262144 | tf_op jit(solution)/shard_map/all_to_all | solution.py:54
  257.4 51.2 %all-gather.9.cloned.1.call-start = ((), (), s32[]{:S(2)}) async-start(), calls=%async_computation.8 | async-start | bytes 3538944 | tf_op jit(solution)/shard_map/all_gather | solution.py:31
  267.6 88.4 %reduce-scatter.17.cloned.1.call-start = ((), (), s32[]{:S(2)}) async-start(), calls=%async_computation.12 | async-start | bytes 2359296
  313.5 103.8 %all-gather.11.cloned.1.call-start = ((), (), s32[]{:S(2)}) async-start(), calls=%async_computation.9 | async-start | bytes 1769472 | tf_op jit(solution)/shard_map/all_gather | solution.py:71
  377.2 40.1 %copy-start.6 = (bf16[2,64,512]{2,1,0:T(8,128)(2,1)S(1)}, bf16[2,64,512]{2,1,0:T(8,128)(2,1)}, u32[]{:S(2)}) copy-start(bf16[2,64,512]{2,1,0:T(8,128)(2,1)} %param.17) | copy-start | bytes 393220
  384.4 76.2 %reduce-scatter.19.cloned.1.call-start = ((), (), s32[]{:S(2)}) async-start(), calls=%async_computation.13 | async-start | bytes 1769472
Sparse Core Ops, SparseCore 0:
  31.5 43.2 all-gather.4
  79.8 42.3 reduce-scatter.12
  150.1 32.8 all-gather.6
  186.9 39.0 reduce-scatter.14
  267.8 40.8 all-gather.8
  313.6 42.4 reduce-scatter.16
  384.5 32.7 all-gather.10
  421.3 39.2 reduce-scatter.18
where the time goes:
time: 488 us; the launch traced here: 487 us
  waiting for transfers between devices  317 us (65%)
  blocking collectives  69.1 us (14%)
  local copies, waits for them, and re-layouts  37.9 us (8%)
  other arithmetic  20.9 us (4%)
  starting transfers between devices  17.3 us (4%)
  between operations  14.6 us (3%)
  matrix products  10.2 us (2%)
    unnamed x12, waiting for transfers between devices  163 us
    all_gather x2, waiting for transfers between devices, edge_hidden(): lax.all_gather(stacked, 'ch', axis=1, tiled=True)  84.3 us
    psum x4, blocking collectives, finish(): lax.psum((jnp.sum(summed, axis=0), jnp.sum(summed * summed, axis=0)), 'ch')  69.1 us
    all_gather x2, waiting for transfers between devices, shards(): lax.all_gather(both, 'ch', axis=1, tiled=True)  65.8 us
    all_to_all x2, starting transfers between devices, shards(): lax.all_to_all(packed, 'dom', split_axis=1, concat_axis=1, tiled=True)  16.9 us
    unnamed x34, local copies, waits for them, and re-layouts  16.5 us
    gather x6, local copies, waits for them, and re-layouts, shards(): stacked = jnp.stack([edges, extended[:, edge_src], nodes[:, edge_dst]])  13.1 us
    scatter-add x2, other arithmetic, shards(): gathered = jnp.zeros((share, node_count), jnp.float32).at[:, edge_dst].ad...  12.3 us
  transfers between devices with their start and end apart: 10, of which 10 were waited for; matrix products, arithmetic and copies ran while one was open for 2% of the time, Pallas kernels for 0%

commit v1 on v0

--- a/solution.py
+++ b/solution.py
@@ -25,11 +25,15 @@
 
 
 def edge_hidden(stacked, weight_in):
+
+    def _turn_cards(z, comm_axis, d0=1):
+        block_now = lax.axis_size(comm_axis)
+        lower = jnp.stack(block_now * [z])
+        shaped = lax.all_to_all(lower, axis_name=comm_axis, split_axis=0, concat_axis=0)
+        return jnp.concatenate(shaped, axis=d0)
+
     return jnp.einsum(
-        "akh,ake->he",
-        weight_in,
-        lax.all_gather(stacked, "ch", axis=1, tiled=True),
-        preferred_element_type=jnp.float32,
+        "akh,ake->he", weight_in, _turn_cards(stacked, "ch"), preferred_element_type=jnp.float32
     )
 
 

time: 488 us -> 559 us (1.15)
  blocking collectives: 69.1 us -> 230 us
  waiting for transfers between devices: 317 us -> 223 us
    all_to_all x0 -> x2, blocking collectives: none -> 162 us  [_turn_cards(): lax.all_to_all(lower, axis_name=comm_axis, split_axis=0, concat_axis=0)]
    all_gather x2 -> x0, waiting for transfers between devices: 84.3 us -> none  [edge_hidden(): lax.all_gather(stacked, 'ch', axis=1, tiled=True)]
    unnamed x12 -> x10, waiting for transfers between devices: 163 us -> 153 us
    unnamed x34 -> x44, local copies, waits for them, and re-layouts: 16.5 us -> 19.5 us
    gather x6 -> x4, local copies, waits for them, and re-layouts: 13.1 us -> 12.8 us  [shards(): stacked = jnp.stack([edges, extended[:, edge_src], nodes[:, edge_dst]])]
  transfers between devices with their start and end apart: 10 -> 8, of which waited for: 10 -> 8; matrix products, arithmetic and copies ran while one was open for 2% -> 1% of each run, Pallas kernels for 0% -> 0%
where the time goes in v1:
time: 559 us; the launch traced here: 558 us
  blocking collectives  230 us (41%)
  waiting for transfers between devices  223 us (40%)
  local copies, waits for them, and re-layouts  41.9 us (7%)
  other arithmetic  20.4 us (4%)
  starting transfers between devices  17.1 us (3%)
  between operations  14.6 us (3%)
  matrix products  10.9 us (2%)
    all_to_all x2, blocking collectives, _turn_cards(): lax.all_to_all(lower, axis_name=comm_axis, split_axis=0, concat_axis=0)  162 us
    unnamed x10, waiting for transfers between devices  153 us
    psum x4, blocking collectives, finish(): lax.psum((jnp.sum(summed, axis=0), jnp.sum(summed * summed, axis=0)), 'ch')  68.8 us
    all_gather x2, waiting for transfers between devices, shards(): lax.all_gather(both, 'ch', axis=1, tiled=True)  65.7 us
    unnamed x44, local copies, waits for them, and re-layouts  19.5 us
    all_to_all x2, starting transfers between devices, shards(): lax.all_to_all(packed, 'dom', split_axis=1, concat_axis=1, tiled=True)  16.8 us
    gather x4, local copies, waits for them, and re-layouts, shards(): stacked = jnp.stack([edges, extended[:, edge_src], nodes[:, edge_dst]])  12.8 us
    scatter-add x2, other arithmetic, shards(): gathered = jnp.zeros((share, node_count), jnp.float32).at[:, edge_dst].ad...  12.3 us
  transfers between devices with their start and end apart: 8, of which 8 were waited for; matrix products, arithmetic and copies ran while one was open for 1% of the time, Pallas kernels for 0%

profile of v1, /device:TPU:42, one launch (start us, length us, event | category | flops | bytes accessed | tf_op | source)
XLA Modules:
  0.0 557.9 jit_solution(8208312749045597225)
XLA Ops:
  7.2 0.7 fusion.44
  7.9 1.1 copy.23
  9.0 3.2 gather_fusion
  12.2 0.8 reshape.136
  13.0 8.4 %all-to-all-start = ((bf16[32,2,1024]{2,1,0:T(2,128)(2,1)}), bf16[32,2,1024]{2,1,0:T(2,128)(2,1)S(1)}, u32[]{:S(2)}, u32[]{:S(2)}) async-start(bf16[32,2,1024]{2,1,0:T(2,128)(2,1)} %reshape.136), calls=%async_computation | async-start | bytes 262144 | tf_op jit(solution)/shard_map/all_to_all | solution.py:58
  21.8 3.2 gather_fusion.2
  25.0 1.9 all-to-all-done
  26.9 0.2 reshape.137
  27.2 3.2 gather_fusion.1
  30.7 0.3 copy.29
  30.9 0.4 stack.69
  31.3 81.9 %all_to_all.20 = bf16[8,3,64,1024]{3,2,1,0:T(8,128)(2,1)S(1)} all-to-all(bf16[8,3,64,1024]{3,2,1,0:T(8,128)(2,1)S(1)} %stack.69), channel_id=1, replica_groups=mesh['dom'=32,'ch'=8] {'ch'}, dimensions={0} | all-to-all | bytes 6291456 | tf_op jit(solution)/shard_map/all_to_all | solution.py:32
  113.2 0.4 copy.30
  113.7 0.5 copy-done.7
  114.1 3.2 convolution_bitcast_fusion.1
  117.4 2.9 copy.38
  120.4 37.4 %reduce-scatter.13.cloned.1.call-done = f32[64,1024]{1,0:T(8,128)} async-done(((f32[512,1024]{1,0:T(8,128)}), f32[64,1024]{1,0:T(8,128)}) %reduce-scatter.13.cloned.1.call-update) | async-done | bytes 262160
  157.9 1.1 copy.39
  159.0 0.2 multiply_reduce_fusion.1
  159.2 1.0 reduce_sum.72
  160.2 18.2 %all-reduce.3 = (f32[1024]{0:T(1024)S(1)}, f32[1024]{0:T(1024)S(1)}) all-reduce(f32[1024]{0:T(1024)S(1)} %multiply_reduce_fusion.1, f32[1024]{0:T(1024)S(1)} %reduce_sum.72), channel_id=1, replica_groups=mesh['dom'=32,'ch'=8] {'ch'}, use_global_device_ids=true, to_apply=%region_4.5 | all-reduce | flops 2048 | bytes 16384 | tf_op jit(solution)/shard_map/psum | solution.py:20
  178.5 0.3 add_convert_fusion
  178.8 6.2 %scatter_custom_fusion = f32[64,768]{0,1:T(8,128)S(1)} fusion(s32[1024]{0:T(1024)S(1)} %get-tuple-element.23, bf16[64,1024]{0,1:T(8,128)(2,1)S(1)} %add_convert_fusion, f32[]{:T(128)} %constant.23.clone.1), kind=kCustom, calls=%fused_computation.22 | custom fusion | flops 131072 | bytes 458756 | tf_op jit(solution)/shard_map/scatter-add | solution.py:68
  185.1 0.7 pad_maximum_fusion.5
  185.9 32.7 %all-gather.3.cloned.1.call-done = bf16[2,512,768]{2,1,0:T(8,128)(2,1)} async-done(((bf16[2,64,768]{2,1,0:T(8,128)(2,1)}), bf16[2,512,768]{2,1,0:T(8,128)(2,1)}) %all-gather.3.cloned.1.call-update) | async-done | bytes 1572880 | tf_op jit(solution)/shard_map/all_gather | solution.py:75
  218.6 2.2 convolution_bitcast_fusion.3
  220.8 1.6 copy.40
  222.5 39.2 %reduce-scatter.15.cloned.1.call-done = f32[64,768]{1,0:T(8,128)} async-done(((f32[512,768]{1,0:T(8,128)}), f32[64,768]{1,0:T(8,128)}) %reduce-scatter.15.cloned.1.call-update) | async-done | bytes 196624
  261.7 1.1 copy.41
  263.0 1.0 reduce_sum.74
  263.9 16.3 %all-reduce.2 = (f32[768]{0:T(1024)S(1)}, f32[768]{0:T(1024)S(1)}) all-reduce(f32[768]{0:T(1024)S(1)} %multiply_reduce_fusion.3, f32[768]{0:T(1024)S(1)} %reduce_sum.74), channel_id=1, replica_groups=mesh['dom'=32,'ch'=8] {'ch'}, use_global_device_ids=true, to_apply=%region_10.11 | all-reduce | flops 1536 | bytes 12288 | tf_op jit(solution)/shard_map/psum | solution.py:20
  280.2 0.3 add_convert_fusion.2
  280.5 3.2 gather_fusion.3
  283.7 0.8 reshape.138
  284.6 8.4 %all-to-all-start.2 = ((bf16[32,2,1024]{2,1,0:T(2,128)(2,1)}), bf16[32,2,1024]{2,1,0:T(2,128)(2,1)S(1)}, u32[]{:S(2)}, u32[]{:S(2)}) async-start(bf16[32,2,1024]{2,1,0:T(2,128)(2,1)} %reshape.138), calls=%async_computation.2 | async-start | bytes 262144 | tf_op jit(solution)/shard_map/all_to_all | solution.py:58
  293.0 3.2 gather_fusion.5
  296.3 2.2 all-to-all-done.2
  298.4 0.2 reshape.139
  298.7 3.2 gather_fusion.4
  302.2 0.3 copy.32
  302.4 0.4 stack.77
  302.8 79.8 %all_to_all.21 = bf16[8,3,64,1024]{3,2,1,0:T(8,128)(2,1)S(1)} all-to-all(bf16[8,3,64,1024]{3,2,1,0:T(8,128)(2,1)S(1)} %stack.77), channel_id=1, replica_groups=mesh['dom'=32,'ch'=8] {'ch'}, dimensions={0} | all-to-all | bytes 6291456 | tf_op jit(solution)/shard_map/all_to_all | solution.py:32
  382.6 0.4 copy.33
  383.0 0.5 copy-done.8
  383.5 3.2 convolution_bitcast_fusion
  386.8 2.9 copy.42
  389.8 37.6 %reduce-scatter.17.cloned.1.call-done = f32[64,1024]{1,0:T(8,128)} async-done(((f32[512,1024]{1,0:T(8,128)}), f32[64,1024]{1,0:T(8,128)}) %reduce-scatter.17.cloned.1.call-update) | async-done | bytes 262160
  427.4 1.1 copy.43
  428.5 0.2 multiply_reduce_fusion
  428.8 1.0 reduce_sum.76
  429.8 17.9 %all-reduce.1 = (f32[1024]{0:T(1024)S(1)}, f32[1024]{0:T(1024)S(1)}) all-reduce(f32[1024]{0:T(1024)S(1)} %multiply_reduce_fusion, f32[1024]{0:T(1024)S(1)} %reduce_sum.76), channel_id=1, replica_groups=mesh['dom'=32,'ch'=8] {'ch'}, use_global_device_ids=true, to_apply=%region_15.16 | all-reduce | flops 2048 | bytes 16384 | tf_op jit(solution)/shard_map/psum | solution.py:20
  447.7 0.3 fusion.6
  448.1 6.2 %scatter_custom_fusion.1 = f32[64,768]{0,1:T(8,128)S(1)} fusion(s32[1024]{0:T(1024)S(1)} %get-tuple-element.23, bf16[64,1024]{0,1:T(8,128)(2,1)S(1)} %fusion.6, f32[]{:T(128)} %constant.23.clone.1), kind=kCustom, calls=%fused_computation.24 | custom fusion | flops 131072 | bytes 458756 | tf_op jit(solution)/shard_map/scatter-add | solution.py:68
  454.3 0.9 copy.34
  455.3 33.0 %all-gather.5.cloned.1.call-done = bf16[2,512,768]{2,0,1:T(2,128)(2,1)} async-done(((bf16[2,64,768]{2,0,1:T(2,128)(2,1)}), bf16[2,512,768]{2,0,1:T(2,128)(2,1)}) %all-gather.5.cloned.1.call-update) | async-done | bytes 1572880 | tf_op jit(solution)/shard_map/all_gather | solution.py:75
  488.2 2.2 convolution_bitcast_fusion.2
  490.5 1.6 copy.44
  492.1 0.8 copy.37
  492.9 38.5 %reduce-scatter.19.cloned.1.call-done = f32[64,768]{1,0:T(8,128)} async-done(((f32[512,768]{1,0:T(8,128)}), f32[64,768]{1,0:T(8,128)}) %reduce-scatter.19.cloned.1.call-update) | async-done | bytes 196624
  531.4 1.1 copy.45
  532.6 1.0 reduce_sum.78
  533.6 16.4 %all-reduce = (f32[768]{0:T(1024)S(1)}, f32[768]{0:T(1024)S(1)}) all-reduce(f32[768]{0:T(1024)S(1)} %multiply_reduce_fusion.2, f32[768]{0:T(1024)S(1)} %reduce_sum.78), channel_id=1, replica_groups=mesh['dom'=32,'ch'=8] {'ch'}, use_global_device_ids=true, to_apply=%region_21.22 | all-reduce | flops 1536 | bytes 12288 | tf_op jit(solution)/shard_map/psum | solution.py:20
  550.0 0.3 add_convert_fusion.1
  550.3 0.8 copy.36
  (54 shorter events, 1.8 us)
Async XLA Ops:
  7.2 14.4 %copy-start.12 = (s32[1024]{0:T(1024)S(1)}, s32[1024]{0:T(1024)}, u32[]{:S(2)}) copy-start(s32[1024]{0:T(1024)} %param.13) | copy-start | bytes 12292
  7.2 14.4 %copy-start.9 = (bf16[64,1024]{1,0:T(8,128)(2,1)S(1)}, bf16[64,1024]{1,0:T(8,128)(2,1)}, u32[]{:S(2)}) copy-start(bf16[64,1024]{1,0:T(8,128)(2,1)} %param.10) | copy-start | bytes 393220
  7.2 17.8 %copy-start.13 = (s32[1024]{0:T(1024)S(1)}, s32[1024]{0:T(1024)}, u32[]{:S(2)}) copy-start(s32[1024]{0:T(1024)} %param.12) | copy-start | bytes 12292
  13.0 13.9 %all-to-all-start = ((bf16[32,2,1024]{2,1,0:T(2,128)(2,1)}), bf16[32,2,1024]{2,1,0:T(2,128)(2,1)S(1)}, u32[]{:S(2)}, u32[]{:S(2)}) async-start(bf16[32,2,1024]{2,1,0:T(2,128)(2,1)} %reshape.136), calls=%async_computation | async-start | bytes 262144 | tf_op jit(solution)/shard_map/all_to_all | solution.py:58
  21.5 136.4 %reduce-scatter.13.cloned.1.call-start = ((), (), s32[]{:S(2)}) async-start(), calls=%async_computation.10 | async-start | bytes 2359296
  21.7 8.9 %copy-start.2 = (bf16[64,1024]{0,1:T(8,128)(2,1)}, bf16[64,1024]{0,1:T(8,128)(2,1)S(1)}, u32[]{:S(2)}) copy-start(bf16[64,1024]{0,1:T(8,128)(2,1)S(1)} %copy.24) | copy-start | bytes 393220
  113.2 0.9 copy-start.7
  120.3 58.1 %copy-start.3 = (bf16[64,1024]{0,1:T(8,128)(2,1)S(1)}, bf16[64,1024]{0,1:T(8,128)(2,1)}, u32[]{:S(2)}) copy-start(bf16[64,1024]{0,1:T(8,128)(2,1)} %copy-done.2) | copy-start | bytes 393220
  120.4 64.8 %copy-start.4 = (bf16[64,768]{1,0:T(8,128)(2,1)S(1)}, bf16[64,768]{1,0:T(8,128)(2,1)}, u32[]{:S(2)}) copy-start(bf16[64,768]{1,0:T(8,128)(2,1)} %param.9) | copy-start | bytes 294916
  120.4 98.2 %copy-start.5 = (bf16[2,2,512,64]{2,3,1,0:T(8,128)(2,1)S(1)}, bf16[2,2,512,64]{2,3,1,0:T(8,128)(2,1)}, u32[]{:S(2)}) copy-start(bf16[2,2,512,64]{2,3,1,0:T(8,128)(2,1)} %param.16) | copy-start | bytes 786436
  120.4 98.2 %copy-start.10 = (bf16[2,64,512]{2,1,0:T(8,128)(2,1)S(1)}, bf16[2,64,512]{2,1,0:T(8,128)(2,1)}, u32[]{:S(2)}) copy-start(bf16[2,64,512]{2,1,0:T(8,128)(2,1)} %param.17) | copy-start | bytes 393220
  120.4 98.2 %all-gather.3.cloned.1.call-start = ((), (), s32[]{:S(2)}) async-start(), calls=%async_computation.8 | async-start | bytes 1769472 | tf_op jit(solution)/shard_map/all_gather | solution.py:75
  178.8 123.1 %copy-start = (bf16[64,1024]{0,1:T(8,128)(2,1)}, bf16[64,1024]{0,1:T(8,128)(2,1)S(1)}, u32[]{:S(2)}) copy-start(bf16[64,1024]{0,1:T(8,128)(2,1)S(1)} %add_convert_fusion) | copy-start | bytes 393220
  185.8 75.9 %reduce-scatter.15.cloned.1.call-start = ((), (), s32[]{:S(2)}) async-start(), calls=%async_computation.11 | async-start | bytes 1769472
  284.6 13.8 %all-to-all-start.2 = ((bf16[32,2,1024]{2,1,0:T(2,128)(2,1)}), bf16[32,2,1024]{2,1,0:T(2,128)(2,1)S(1)}, u32[]{:S(2)}, u32[]{:S(2)}) async-start(bf16[32,2,1024]{2,1,0:T(2,128)(2,1)} %reshape.138), calls=%async_computation.2 | async-start | bytes 262144 | tf_op jit(solution)/shard_map/all_to_all | solution.py:58
  293.0 134.4 %reduce-scatter.17.cloned.1.call-start = ((), (), s32[]{:S(2)}) async-start(), calls=%async_computation.12 | async-start | bytes 2359296
  382.6 0.9 copy-start.8
  389.7 58.0 %copy-start.1 = (bf16[64,1024]{0,1:T(8,128)(2,1)S(1)}, bf16[64,1024]{0,1:T(8,128)(2,1)}, u32[]{:S(2)}) copy-start(bf16[64,1024]{0,1:T(8,128)(2,1)} %copy-done) | copy-start | bytes 393220
  389.7 98.5 %all-gather.5.cloned.1.call-start = ((), (), s32[]{:S(2)}) async-start(), calls=%async_computation.9 | async-start | bytes 1769472 | tf_op jit(solution)/shard_map/all_gather | solution.py:75
  428.8 59.5 %copy-start.6 = (bf16[2,2,512,64]{2,3,1,0:T(8,128)(2,1)S(1)}, bf16[2,2,512,64]{2,3,1,0:T(8,128)(2,1)}, u32[]{:S(2)}) copy-start(bf16[2,2,512,64]{2,3,1,0:T(8,128)(2,1)} %param.16) | copy-start | bytes 786436
  428.8 59.5 %copy-start.11 = (bf16[2,64,512]{2,1,0:T(8,128)(2,1)S(1)}, bf16[2,64,512]{2,1,0:T(8,128)(2,1)}, u32[]{:S(2)}) copy-start(bf16[2,64,512]{2,1,0:T(8,128)(2,1)} %param.17) | copy-start | bytes 393220
  455.2 76.1 %reduce-scatter.19.cloned.1.call-start = ((), (), s32[]{:S(2)}) async-start(), calls=%async_computation.13 | async-start | bytes 1769472
Sparse Core Ops, SparseCore 0:
  120.5 37.3 reduce-scatter.12
  186.0 32.6 all-gather.2
  222.6 39.0 reduce-scatter.14
  389.8 37.4 reduce-scatter.16
  455.3 32.8 all-gather.4
  492.2 39.0 reduce-scatter.18
